TPU v7x, 1024 devices: a whole 4x4x32 slice. The times are simulated.
1024 devices in a mesh: group: 8 (over x, z_hi), tp: 16 (over z_lo), dp: 8 (over y, core).
Axes of the slice: x: 4, y: 4, z: 32 (z_hi: 2, z_lo: 16; z = z_hi * 16 + z_lo), core: 2. Of those that a mesh axis runs over, the one named last changes fastest.
Arguments:
- image_slots: bfloat16 [2048, 8192], P(('group', 'tp'), 'dp'), may hold values from -6 to 6
- image_cot: bfloat16 [2048, 8192], P(('group', 'tp'), 'dp'), may hold values from -6 to 6
- text_rows: bfloat16 [1024, 8192], P(('group', 'tp'), 'dp'), may hold values from -6 to 6
- text_cot: bfloat16 [1024, 8192], P(('group', 'tp'), 'dp'), may hold values from -6 to 6
- destination: int32 [1024, 1], P(('group', 'tp')), may hold values from 0 to 7; in each aligned block of 8 rows (0 to 7, 8 to 15, ...) at most 2 rows name the same one
- text_count: int32 [128], P(('group', 'tp')), may hold values from 1 to 8, 768 in all
- w_gate: bfloat16 [8192, 14336], P('dp', 'tp'), may hold values from -0.0625 to 0.0625
- w_up: bfloat16 [8192, 14336], P('dp', 'tp'), may hold values from -0.0625 to 0.0625
- w_down: bfloat16 [14336, 8192], P('tp', 'dp'), may hold values from -0.046875 to 0.046875
Outputs:
- image_grad: bfloat16 [1024, 8192], P(('group', 'tp'), 'dp')
- text_grad: bfloat16 [1024, 8192], P(('group', 'tp'), 'dp')
Inputs may be any that keep to these rules, and one draw needn't show every extreme that they name: In the rows of one block of 8 rows no group is named more than 2 times, and some block names one group exactly 2 times; destination[i] decides which slot of image_slots and image_cot holds row i. Each block of 8 text rows has text_count live rows first; some block is full.
All inputs are finite; a program needn't handle non-finite values.
Results may differ from a plain program's by a relative error of at most 0.025.
Values may be sent and summed in bfloat16 or wider, within the bound.
A program may use at most 32 MiB of HBM per device.

v0:
```python
import jax
import jax.numpy as jnp
from jax import lax
from jax.sharding import PartitionSpec as P


def laid_out(tiles, dim):
    tiles = jnp.moveaxis(tiles, 0, dim)
    shape = tiles.shape
    return tiles.reshape(*shape[:dim], shape[dim] * shape[dim + 1], *shape[dim + 2 :])


def copy_for_each(value, axis):
    peers = lax.axis_size(axis)
    return lax.all_to_all(
        jnp.broadcast_to(value[None], (peers, *value.shape)), axis, 0, 0, tiled=True
    )


def collect(value, axis, dim):
    return laid_out(copy_for_each(value, axis), dim)


def split_up(value, dim, peers):
    before, after = (value.shape[:dim], value.shape[dim + 1 :])
    return jnp.moveaxis(value.reshape(*before, peers, -1, *after), dim, 0)


def summed_on_arrival(value, axis, dim):
    tiles = split_up(value, dim, lax.axis_size(axis))
    arrived = lax.all_to_all(tiles, axis, split_axis=0, concat_axis=0, tiled=True)
    return arrived.astype(jnp.float32).sum(axis=0)


def language_grads(combined, w_gate, w_up, w_down):
    feat_dev = w_gate.shape[0]
    hidden_dev = w_gate.shape[1]
    piece = collect(combined, "tp", 0)
    inputs_part = piece[:, :feat_dev]
    cot_part = piece[:, feat_dev:]
    gate = jnp.dot(inputs_part, w_gate, preferred_element_type=jnp.float32)
    up = jnp.dot(inputs_part, w_up, preferred_element_type=jnp.float32)
    back = lax.dot_general(
        cot_part, w_down, (((1,), (1,)), ((), ())), preferred_element_type=jnp.float32
    )
    partial_value = jnp.concatenate([gate, up, back], axis=1)
    sums = summed_on_arrival(partial_value.astype(jnp.bfloat16), "dp", 0)
    gate = sums[:, :hidden_dev]
    up = sums[:, hidden_dev : 2 * hidden_dev]
    back = sums[:, 2 * hidden_dev :]
    sigmoid_gate = jax.nn.sigmoid(gate)
    dgate = (back * up * sigmoid_gate * (1.0 + gate * (1.0 - sigmoid_gate))).astype(jnp.bfloat16)
    dup = (back * gate * sigmoid_gate).astype(jnp.bfloat16)
    stacked = jnp.concatenate([dgate, dup], axis=1)
    piece = collect(stacked, "dp", 0)
    total = lax.dot_general(
        piece[:, :hidden_dev], w_gate, (((1,), (1,)), ((), ())), preferred_element_type=jnp.float32
    )
    terms = total + lax.dot_general(
        piece[:, hidden_dev:], w_up, (((1,), (1,)), ((), ())), preferred_element_type=jnp.float32
    )
    return summed_on_arrival(terms.astype(jnp.bfloat16), "tp", 0).astype(jnp.bfloat16)


def per_device(
    image_slots, image_cot, text_rows, text_cot, destination, text_count, w_gate, w_up, w_down
):
    groups = lax.axis_size("group")
    slot_dev = image_slots.shape[0]
    capacity = slot_dev // groups
    image_dev = destination.shape[0]
    text_dev = text_rows.shape[0]
    target = destination[:, 0]
    position = lax.broadcasted_iota(jnp.int32, (image_dev, image_dev), 0)
    other = lax.broadcasted_iota(jnp.int32, (image_dev, image_dev), 1)
    same = (target[:, None] == target[None, :]) & (other < position)
    rank = jnp.sum(same.astype(jnp.int32), axis=1)
    column = target * capacity + rank
    slot_index = lax.broadcasted_iota(jnp.int32, (image_dev, slot_dev), 1)
    select = (column[:, None] == slot_index).astype(jnp.bfloat16)
    text_both = jnp.concatenate([text_rows, text_cot], axis=1)
    both = jnp.concatenate([image_slots, image_cot], axis=1)
    arrived = lax.all_to_all(both, "group", split_axis=0, concat_axis=0, tiled=True)
    picked = jnp.dot(select, arrived, preferred_element_type=jnp.float32).astype(jnp.bfloat16)
    combined = jnp.concatenate([picked, text_both], axis=0)
    grads = language_grads(combined, w_gate, w_up, w_down)
    image_grad = grads[:image_dev]
    text_part = grads[image_dev:]
    live = lax.broadcasted_iota(jnp.int32, (text_dev, 1), 0) < text_count[0]
    text_grad = jnp.where(live, text_part, jnp.zeros_like(text_part))
    return (image_grad, text_grad)


def solution(mesh):
    placed = (
        P(("group", "tp"), "dp"),
        P(("group", "tp"), "dp"),
        P(("group", "tp"), "dp"),
        P(("group", "tp"), "dp"),
        P(("group", "tp"), None),
        P(("group", "tp")),
        P("dp", "tp"),
        P("dp", "tp"),
        P("tp", "dp"),
    )
    return jax.shard_map(
        per_device,
        mesh=mesh,
        in_specs=placed,
        out_specs=(P(("group", "tp"), "dp"), P(("group", "tp"), "dp")),
        check_vma=False,
    )
```

profile of v0, /device:TPU:24, one launch (start us, length us, event | category | flops | bytes accessed | tf_op | source)
XLA Modules:
  0.0 274.4 jit_solution(609086798244848024)
XLA Ops:
  0.6 0.0 copy-start
  0.6 0.9 pad_maximum_fusion.2
  1.6 0.7 all_to_all.20
  2.2 30.8 %all-to-all-start = ((bf16[8,2,2048]{2,1,0:T(2,128)(2,1)}), bf16[8,2,2048]{2,1,0:T(2,128)(2,1)S(1)}, u32[]{:S(2)}, u32[]{:S(2)}) async-start(bf16[8,2,2048]{2,1,0:T(2,128)(2,1)} %all_to_all.20), calls=%async_computation | async-start | bytes 131072 | tf_op jit(solution)/shard_map/all_to_all | solution.py:83
  33.0 0.9 convert_reduce_fusion.1
  33.9 0.7 fusion.12
  34.6 23.1 %all-to-all-done = bf16[8,2,2048]{2,1,0:T(2,128)(2,1)S(1)} async-done(((bf16[8,2,2048]{2,1,0:T(2,128)(2,1)}), bf16[8,2,2048]{2,1,0:T(2,128)(2,1)S(1)}, u32[]{:S(2)}, u32[]{:S(2)}) %all-to-all-start) | async-done | bytes 65568 | tf_op jit(solution)/shard_map/all_to_all | solution.py:83
  57.7 0.2 convolution_convert_fusion
  57.9 0.7 maximum_maximum_fusion
  58.7 0.1 broadcast_in_dim.11
  58.8 105.8 %all_to_all.32 = bf16[16,16,2048]{2,1,0:T(8,128)(2,1)S(1)} all-to-all(bf16[16,16,2048]{2,1,0:T(8,128)(2,1)S(1)} %broadcast_in_dim.11), channel_id=1, replica_groups=mesh['group'=8,'tp'=16,'dp'=8] {'tp'}, dimensions={0} | all-to-all | bytes 2097152 | tf_op jit(solution)/shard_map/all_to_all | solution.py:15
  164.5 0.0 copy-start.1
  164.5 0.0 copy-done
  164.6 0.7 convolution_convert_fusion.3
  165.3 0.8 copy-done.1
  166.0 0.0 copy-start.2
  166.0 0.7 convolution_convert_fusion.2
  166.8 0.8 copy-done.2
  167.5 0.7 convolution_convert_fusion.1
  168.3 0.1 pad_maximum_fusion
  168.4 21.9 %all_to_all.33 = bf16[8,32,2688]{2,1,0:T(8,128)(2,1)S(1)} all-to-all(bf16[8,32,2688]{2,1,0:T(8,128)(2,1)S(1)} %pad_maximum_fusion), channel_id=1, replica_groups=mesh['group'=8,'tp'=16,'dp'=8] {'dp'}, dimensions={0} | all-to-all | bytes 2752512 | tf_op jit(solution)/shard_map/all_to_all | solution.py:31
  190.3 0.2 convert_reduce_fusion
  190.5 0.1 fusion.9
  190.6 0.1 broadcast_in_dim.12
  190.7 17.0 %all_to_all.34 = bf16[8,32,1792]{2,1,0:T(8,128)(2,1)S(1)} all-to-all(bf16[8,32,1792]{2,1,0:T(8,128)(2,1)S(1)} %broadcast_in_dim.12), channel_id=1, replica_groups=mesh['group'=8,'tp'=16,'dp'=8] {'dp'}, dimensions={0} | all-to-all | bytes 1835008 | tf_op jit(solution)/shard_map/all_to_all | solution.py:15
  207.6 0.7 fusion.5
  208.4 1.5 fusion
  209.9 10.4 %all-to-all-start.4 = ((bf16[16,16,1024]{2,1,0:T(8,128)(2,1)}), bf16[16,16,1024]{2,1,0:T(8,128)(2,1)S(1)}, u32[]{:S(2)}, u32[]{:S(2)}) async-start(bf16[16,16,1024]{2,1,0:T(8,128)(2,1)} %bitcast.8), calls=%async_computation.4 | async-start | bytes 1048576 | tf_op jit(solution)/shard_map/all_to_all | solution.py:31
  221.0 52.6 %all-to-all-done.4 = bf16[16,16,1024]{2,1,0:T(8,128)(2,1)S(1)} async-done(((bf16[16,16,1024]{2,1,0:T(8,128)(2,1)}), bf16[16,16,1024]{2,1,0:T(8,128)(2,1)S(1)}, u32[]{:S(2)}, u32[]{:S(2)}) %all-to-all-start.4) | async-done | bytes 524320 | tf_op jit(solution)/shard_map/all_to_all | solution.py:31
  273.6 0.1 reduce_sum.35
  273.7 0.7 slice_select_fusion
  (3 shorter events, 0.0 us)
Async XLA Ops:
  0.6 163.9 %copy-start = (bf16[1024,896]{1,0:T(8,128)(2,1)S(1)}, bf16[1024,896]{1,0:T(8,128)(2,1)}, u32[]{:S(2)}) copy-start(bf16[1024,896]{1,0:T(8,128)(2,1)} %param.15) | copy-start | bytes 5505028
  2.2 55.5 %all-to-all-start = ((bf16[8,2,2048]{2,1,0:T(2,128)(2,1)}), bf16[8,2,2048]{2,1,0:T(2,128)(2,1)S(1)}, u32[]{:S(2)}, u32[]{:S(2)}) async-start(bf16[8,2,2048]{2,1,0:T(2,128)(2,1)} %all_to_all.20), calls=%async_computation | async-start | bytes 131072 | tf_op jit(solution)/shard_map/all_to_all | solution.py:83
  164.5 1.5 copy-start.1
  166.0 1.5 copy-start.2
  209.9 63.7 %all-to-all-start.4 = ((bf16[16,16,1024]{2,1,0:T(8,128)(2,1)}), bf16[16,16,1024]{2,1,0:T(8,128)(2,1)S(1)}, u32[]{:S(2)}, u32[]{:S(2)}) async-start(bf16[16,16,1024]{2,1,0:T(8,128)(2,1)} %bitcast.8), calls=%async_computation.4 | async-start | bytes 1048576 | tf_op jit(solution)/shard_map/all_to_all | solution.py:31
where the time goes:
time: 276 us; the launch traced here: 274 us
  blocking collectives  145 us (53%)
  waiting for transfers between devices  75.7 us (27%)
  starting transfers between devices  41.2 us (15%)
  matrix products  4.66 us (2%)
  other arithmetic  4.36 us (2%)
    all_to_all x2, blocking collectives, copy_for_each(): lax.all_to_all(jnp.broadcast_to(value[None], (peers, *value.shape)), axis...  123 us
    all_to_all x1, waiting for transfers between devices, summed_on_arrival(): lax.all_to_all(tiles, axis, split_axis=0, concat_axis=0, tiled=True)  52.6 us
    all_to_all x1, starting transfers between devices, per_device(): lax.all_to_all(both, 'group', split_axis=0, concat_axis=0, tiled=True)  30.8 us
    all_to_all x1, waiting for transfers between devices, per_device(): lax.all_to_all(both, 'group', split_axis=0, concat_axis=0, tiled=True)  23.1 us
    all_to_all x1, blocking collectives, summed_on_arrival(): lax.all_to_all(tiles, axis, split_axis=0, concat_axis=0, tiled=True)  21.9 us
    all_to_all x1, starting transfers between devices, summed_on_arrival(): lax.all_to_all(tiles, axis, split_axis=0, concat_axis=0, tiled=True)  10.4 us
  transfers between devices with their start and end apart: 2, of which 2 were waited for; matrix products, arithmetic and copies ran while one was open for 1% of the time, Pallas kernels for 0%

commit v1 on v0

v1 whole, which is shorter than its diff:
```python
import functools

import jax
import jax.numpy as jnp
from jax import lax
from jax.experimental import pallas as pl
from jax.experimental.pallas import tpu as pltpu
from jax.sharding import PartitionSpec as P

MESH = pl.DeviceIdType.MESH
F32 = jnp.float32
BF16 = jnp.bfloat16
ROWS = 8
KINDS = 3


def kernel(
    nx, nt, ny, cap, feat, hid,
    cand_ref, text_ref, col_ref, live_ref, wg_ref, wu_ref, wd_ref,
    img_ref, txt_ref,
    wg, wu, wd, xr, mix, tb, ib, xs, cs, part, mate, summed, parts_in, grads, ds, terms,
    ra_l, ra_r, sa_l, sa_r, far_a, far_a_in,
    rn_l, rn_r, sn_l, sn_r, rf_l, rf_r, sf_l, sf_r,
    wsem, xs_s, xs_r, hop_s, hop_r, mate_s, mate_r, y_s, y_r, ag_s, ag_r, fw_s, fw_r,
    a_s, a_r, b_s, b_r, f_s, f_r,
):
    ring = 2 * nt
    right_hops, left_hops = nt // 2, nt // 2 - 1
    half = nt // 4
    own = right_hops
    g, t, d = lax.axis_index("group"), lax.axis_index("tp"), lax.axis_index("dp")
    x, z, y, c = g // 2, (g % 2) * nt + t, d // 2, d % 2

    def at(dx=0, dz=0, dy=0, flip=False):
        zz = lax.rem(z + dz + ring, ring)
        xx = lax.rem(x + dx, nx)
        yy = lax.rem(y + dy, ny)
        cc = 1 - c if flip else c
        return {"group": xx * 2 + zz // nt, "tp": lax.rem(zz, nt), "dp": yy * 2 + cc}

    started = []

    def send(src, dst, s, r, device):
        copy = pltpu.make_async_remote_copy(
            src, dst, s, r, device_id=device, device_id_type=MESH
        )
        copy.start()
        started.append(copy)
        return copy

    loads = [
        pltpu.make_async_copy(a, b, wsem.at[i])
        for i, (a, b) in enumerate(((wg_ref, wg), (wu_ref, wu), (wd_ref, wd)))
    ]
    for load in loads:
        load.start()

    peers = [at(dx=i) for i in range(1, nx)]
    peers += [at(dy=i) for i in range(1, ny)]
    peers += [at(flip=True), at(dz=1), at(dz=-1)]
    far_steps = (-(half + 1), half, 2 * half, -(2 * half + 1), nt)
    for step in far_steps:
        peers += [at(dz=step)]
        if step != nt:
            peers += [at(dz=-step)]
    barrier = pltpu.get_barrier_semaphore()
    for peer in peers:
        pl.semaphore_signal(barrier, inc=1, device_id=peer, device_id_type=MESH)
    pl.semaphore_wait(barrier, len(peers))

    xcopies = []
    for i in range(1, nx):
        xcopies.append(
            send(cand_ref.at[lax.rem(x + i, nx)], xr.at[i], xs_s.at[i], xs_r.at[i], at(dx=i))
        )

    flying = {}

    def forward(kind, k, way):
        buf = tb if kind == 0 else ib
        sign = -1 if way == 0 else 1
        src = buf.at[own + sign * (k - 1)]
        if kind == 0 and k == 1:
            src = text_ref
        index = (kind * 2 + way) * right_hops + k - 1
        flying[kind, k, way] = send(
            src, buf.at[own + sign * k], hop_s.at[index], hop_r.at[index],
            at(dz=1 if way == 0 else -1),
        )

    def arrive(k):
        for kind in (0, 1):
            for way in (0, 1):
                last = right_hops if way == 0 else left_hops
                if k <= last:
                    flying[kind, k, way].wait_recv()
                    if k < last:
                        forward(kind, k + 1, way)

    forward(0, 1, 0)
    forward(0, 1, 1)
    for copy in xcopies:
        copy.wait_recv()
    for i in range(nx):
        for rel in range(2):
            piece = cand_ref[x, rel] if i == 0 else xr[i, rel]
            mix[rel, cap * i : cap * i + cap, :] = piece.astype(F32)
    for rel in range(2):
        ib[own, rel] = mix[rel].astype(BF16)
    forward(1, 1, 0)
    forward(1, 1, 1)

    def source_slots(phase):
        if phase == 0:
            return [own - half + j for j in range(2 * half)]
        return [j for j in range(half)] + [own + half + j for j in range(half)]

    def gather_rows(phase):
        slots = source_slots(phase)
        for p in range(half):
            pieces = []
            for s in slots[2 * p : 2 * p + 2]:
                pieces.append((text_ref[...] if s == own else tb[s]).astype(F32))
                pieces.append(ib[s, 0].astype(F32))
                pieces.append(ib[s, 1].astype(F32))
            rows = jnp.concatenate(pieces, axis=0).astype(BF16)
            span = 2 * KINDS * ROWS
            xs[phase, span * p : span * p + span, :] = rows[:, :feat]
            cs[phase, span * p : span * p + span, :] = rows[:, feat:]

    def first_dot(phase, which):
        if which < 2:
            out = jnp.dot(xs[phase], (wg, wu)[which][...], preferred_element_type=F32)
        else:
            out = lax.dot_general(
                cs[phase], wd[...], (((1,), (1,)), ((), ())), preferred_element_type=F32
            )
        for j in range(2 * half):
            block = out[j * KINDS * ROWS : (j + 1) * KINDS * ROWS]
            part[phase, j % 2, j // 2, :, :, which * hid : (which + 1) * hid] = (
                block.reshape(KINDS, ROWS, hid).astype(BF16)
            )

    mates = {}

    def start_mate(phase):
        mates[phase] = send(
            part.at[phase, 1 - c], mate.at[phase], mate_s.at[phase], mate_r.at[phase],
            at(flip=True),
        )

    ysends = {}

    def add_mate(phase):
        mates[phase].wait_recv()
        for i in list(range(1, ny)) + [0]:
            yy = lax.rem(y + i, ny)
            total = part[phase, c, yy].astype(F32) + mate[phase, yy].astype(F32)
            summed[phase, i] = total.astype(BF16)
            if i:
                ysends[phase, i] = send(
                    summed.at[phase, i], parts_in.at[phase, i],
                    y_s.at[phase * ny + i], y_r.at[phase * ny + i], at(dy=i),
                )

    gathers = {}

    def middle(phase):
        for i in range(1, ny):
            ysends[phase, i].wait_recv()
        total = summed[phase, 0].astype(F32)
        for i in range(1, ny):
            total = total + parts_in[phase, i].astype(F32)
        gate, up, back = (total[:, :, i * hid : (i + 1) * hid] for i in range(3))
        s = jax.nn.sigmoid(gate)
        dgate = back * up * s * (1.0 + gate * (1.0 - s))
        dup = back * gate * s
        grads[phase, c, y, :, :, :hid] = dgate.astype(BF16)
        grads[phase, c, y, :, :, hid:] = dup.astype(BF16)
        mine = grads.at[phase, c, y]
        for i in range(1, ny):
            gathers[phase, i] = send(
                mine, mine, ag_s.at[phase * ny + i], ag_r.at[phase * ny + i], at(dy=i)
            )
        gathers[phase, 0] = send(
            mine, mine, fw_s.at[phase * ny], fw_r.at[phase * ny], at(flip=True)
        )

    def pass_on(phase):
        for i in range(1, ny):
            gathers[phase, i].wait_recv()
            theirs = grads.at[phase, c, lax.rem(y - i + ny, ny)]
            gathers[phase, -i] = send(
                theirs, theirs, fw_s.at[phase * ny + i], fw_r.at[phase * ny + i], at(flip=True)
            )

    def second_dots(phase):
        for i in range(ny):
            gathers[phase, -i].wait_recv()
        for p in range(half):
            pieces = []
            for j in (2 * p, 2 * p + 1):
                block = grads[phase, j % 2, j // 2].astype(F32)
                pieces.append(block.reshape(KINDS * ROWS, 2 * hid))
            span = 2 * KINDS * ROWS
            ds[phase, span * p : span * p + span, :] = jnp.concatenate(pieces, axis=0).astype(BF16)
        nt_dims = (((1,), (1,)), ((), ()))
        out = lax.dot_general(ds[phase][:, :hid], wg[...], nt_dims, preferred_element_type=F32)
        out = out + lax.dot_general(
            ds[phase][:, hid:], wu[...], nt_dims, preferred_element_type=F32
        )
        for j in range(2 * half):
            block = out[j * KINDS * ROWS : (j + 1) * KINDS * ROWS]
            terms[phase, j] = block.reshape(KINDS, ROWS, feat).astype(BF16)

    chain = {}

    def chain_a(s):
        if s == 1:
            left, right = terms.at[0, 0], terms.at[0, 2 * half - 1]
        else:
            chain["l", s - 1].wait_recv()
            sa_l[s - 2] = (terms[0, s - 1].astype(F32) + ra_l[s - 2].astype(F32)).astype(BF16)
            left = sa_l.at[s - 2]
            if s <= half - 1:
                chain["r", s - 1].wait_recv()
                sa_r[s - 2] = (
                    terms[0, 2 * half - s].astype(F32) + ra_r[s - 2].astype(F32)
                ).astype(BF16)
                right = sa_r.at[s - 2]
        chain["l", s] = send(left, ra_l.at[s - 1], a_s.at[s - 1], a_r.at[s - 1], at(dz=-1))
        if s <= half - 1:
            n = half + s - 1
            chain["r", s] = send(right, ra_r.at[s - 1], a_s.at[n], a_r.at[n], at(dz=1))

    def finish_a():
        chain["l", half].wait_recv()
        total = terms[0, half].astype(F32) + ra_l[half - 1].astype(F32)
        if half > 1:
            chain["r", half - 1].wait_recv()
            total = total + ra_r[half - 2].astype(F32)
        far_a[...] = total[2].astype(BF16)
        chain["f"] = send(far_a, far_a_in, f_s.at[0], f_r.at[0], at(dz=nt))
        return total[:2]

    def chain_b(s):
        moves = (
            ("nl", rn_l, sn_l, s - 1, slice(0, 2), -1, -(half + 1)),
            ("nr", rn_r, sn_r, 2 * half - s, slice(0, 2), 1, half),
            ("fr", rf_r, sf_r, half - s, slice(2, 3), 1, 2 * half),
            ("fl", rf_l, sf_l, half + s - 1, slice(2, 3), -1, -(2 * half + 1)),
        )
        for i, (name, got, made, j, kinds, step, last) in enumerate(moves):
            if s == 1:
                src = terms.at[1, j, kinds]
            else:
                chain[name, s - 1].wait_recv()
                made[s - 2] = (terms[1, j, kinds].astype(F32) + got[s - 2].astype(F32)).astype(BF16)
                src = made.at[s - 2]
            n = i * half + s - 1
            chain[name, s] = send(
                src, got.at[s - 1], b_s.at[n], b_r.at[n], at(dz=last if s == half else step)
            )

    for k in range(1, half + 1):
        arrive(k)
    gather_rows(0)
    loads[0].wait()
    first_dot(0, 0)
    arrive(half + 1)
    loads[1].wait()
    first_dot(0, 1)
    loads[2].wait()
    first_dot(0, 2)
    start_mate(0)
    for k in range(half + 2, right_hops + 1):
        arrive(k)
        if k == half + 2:
            add_mate(0)
    middle(0)
    gather_rows(1)
    first_dot(1, 0)
    first_dot(1, 1)
    pass_on(0)
    first_dot(1, 2)
    start_mate(1)
    second_dots(0)
    chain_a(1)
    add_mate(1)
    for s in range(2, half):
        chain_a(s)
    middle(1)
    if half > 1:
        chain_a(half)
    pass_on(1)
    near = finish_a()
    mix[0, :, :feat] = near[0]
    mix[1, :, :feat] = near[1]
    second_dots(1)
    for s in range(1, half + 1):
        chain_b(s)
    chain["nl", half].wait_recv()
    chain["nr", half].wait_recv()
    last = rn_l[half - 1].astype(F32) + rn_r[half - 1].astype(F32)
    text = (mix[0, :, :feat] + last[0]).astype(BF16).astype(F32)
    close = (mix[1, :, :feat] + last[1]).astype(BF16).astype(F32)
    txt_ref[...] = jnp.where(live_ref[...] > 0, text, 0.0).astype(BF16)
    chain["f"].wait_recv()
    chain["fr", half].wait_recv()
    chain["fl", half].wait_recv()
    distant = (
        far_a_in[...].astype(F32)
        + rf_r[half - 1, 0].astype(F32)
        + rf_l[half - 1, 0].astype(F32)
    ).astype(BF16).astype(F32)
    chosen = jnp.zeros_like(distant)
    column = col_ref[...]
    for i in range(ROWS):
        chosen = jnp.where(column == i, close[i : i + 1, :], chosen)
        chosen = jnp.where(column == ROWS + i, distant[i : i + 1, :], chosen)
    img_ref[...] = chosen.astype(BF16)
    for copy in started:
        copy.wait_send()


def per_device(
    image_slots, image_cot, text_rows, text_cot, destination, text_count, w_gate, w_up, w_down
):
    groups = lax.axis_size("group")
    nt, ndp = lax.axis_size("tp"), lax.axis_size("dp")
    nx, ny = groups // 2, ndp // 2
    slot_dev, feat = image_slots.shape
    hid = w_gate.shape[1]
    cap = slot_dev // groups
    rows = destination.shape[0]
    g = lax.axis_index("group")
    x, upper = g // 2, g % 2
    target = destination[:, 0]
    position = lax.broadcasted_iota(jnp.int32, (rows, rows), 0)
    other = lax.broadcasted_iota(jnp.int32, (rows, rows), 1)
    same = (target[:, None] == target[None, :]) & (other < position)
    rank = jnp.sum(same.astype(jnp.int32), axis=1)
    away = (target % 2 != upper).astype(jnp.int32)
    column = away * ROWS + (x - target // 2 + nx) % nx * cap + rank
    column = jnp.broadcast_to(column[:, None], (rows, feat))
    live = lax.broadcasted_iota(jnp.int32, (rows, feat), 0) < text_count[0]
    both = jnp.concatenate([image_slots, image_cot], axis=1).reshape(nx, 2, cap, 2 * feat)
    both = jnp.where(upper == 0, both, both[:, ::-1])
    text_both = jnp.concatenate([text_rows, text_cot], axis=1)
    half = nt // 4
    span = 2 * half * KINDS * ROWS
    vm, dma = pltpu.VMEM, pltpu.SemaphoreType.DMA
    block = (KINDS, ROWS, feat)
    hops = nt // 2
    scratch = [
        vm((feat, hid), BF16), vm((feat, hid), BF16), vm((hid, feat), BF16),
        vm((nx, 2, cap, 2 * feat), BF16), vm((2, ROWS, 2 * feat), F32),
        vm((nt, ROWS, 2 * feat), BF16), vm((nt, 2, ROWS, 2 * feat), BF16),
        vm((2, span, feat), BF16), vm((2, span, feat), BF16),
        vm((2, 2, ny, KINDS, ROWS, 3 * hid), BF16), vm((2, ny, KINDS, ROWS, 3 * hid), BF16),
        vm((2, ny, KINDS, ROWS, 3 * hid), BF16), vm((2, ny, KINDS, ROWS, 3 * hid), BF16),
        vm((2, 2, ny, KINDS, ROWS, 2 * hid), BF16), vm((2, span, 2 * hid), BF16),
        vm((2, 2 * half, *block), BF16),
        vm((half, *block), BF16), vm((half, *block), BF16),
        vm((half, *block), BF16), vm((half, *block), BF16),
        vm((ROWS, feat), BF16), vm((ROWS, feat), BF16),
        *[vm((half, 2, ROWS, feat), BF16) for _ in range(4)],
        *[vm((half, 1, ROWS, feat), BF16) for _ in range(4)],
        dma((3,)), dma((nx,)), dma((nx,)), dma((4 * hops,)), dma((4 * hops,)),
        dma((2,)), dma((2,)), dma((2 * ny,)), dma((2 * ny,)), dma((2 * ny,)), dma((2 * ny,)),
        dma((2 * ny,)), dma((2 * ny,)), dma((2 * half,)), dma((2 * half,)),
        dma((4 * half,)), dma((4 * half,)), dma((1,)), dma((1,)),
    ]
    whole = pl.BlockSpec(memory_space=pltpu.VMEM)
    apart = pl.BlockSpec(memory_space=pl.ANY)
    out = jax.ShapeDtypeStruct((ROWS, feat), BF16)
    return pl.pallas_call(
        functools.partial(kernel, nx, nt, ny, cap, feat, hid),
        out_shape=(out, out),
        in_specs=[whole] * 4 + [apart] * 3,
        out_specs=(whole, whole),
        scratch_shapes=scratch,
        compiler_params=pltpu.CompilerParams(
            collective_id=0, has_side_effects=True, vmem_limit_bytes=48 << 20
        ),
    )(both, text_both, column, live.astype(jnp.int32), w_gate, w_up, w_down)


def solution(mesh):
    placed = (
        P(("group", "tp"), "dp"),
        P(("group", "tp"), "dp"),
        P(("group", "tp"), "dp"),
        P(("group", "tp"), "dp"),
        P(("group", "tp"), None),
        P(("group", "tp")),
        P("dp", "tp"),
        P("dp", "tp"),
        P("tp", "dp"),
    )
    return jax.shard_map(
        per_device,
        mesh=mesh,
        in_specs=placed,
        out_specs=(P(("group", "tp"), "dp"), P(("group", "tp"), "dp")),
        check_vma=False,
    )
```

time: 276 us -> 124 us (0.45)
  blocking collectives: 145 us -> 0 us
  Pallas kernels: 0 us -> 113 us
  waiting for transfers between devices: 75.7 us -> 0 us
  starting transfers between devices: 41.2 us -> 0 us
  matrix products: 4.66 us -> 0 us
  local copies, waits for them, and re-layouts: 2.43 us -> 5.91 us
    all_to_all x3 -> x0, blocking collectives: 145 us -> none  [the longest x2 123 us: copy_for_each(): lax.all_to_all(jnp.broadcast_to(value[None], (peers, *value.shape)), axis...]
    pallas_call x0 -> x1, Pallas kernels: none -> 113 us  [per_device(): pl.pallas_call(functools.partial(kernel, nx, nt, ny, cap, feat, hid), out...]
    all_to_all x2 -> x0, waiting for transfers between devices: 75.7 us -> none  [the longest x1 52.6 us: summed_on_arrival(): lax.all_to_all(tiles, axis, split_axis=0, concat_axis=0, tiled=True)]
    all_to_all x2 -> x0, starting transfers between devices: 41.2 us -> none  [the longest x1 30.8 us: per_device(): lax.all_to_all(both, 'group', split_axis=0, concat_axis=0, tiled=True)]
    dot_general x6 -> x0, matrix products: 4.66 us -> none  [the longest x1 1.55 us: language_grads(): lax.dot_general(piece[:, hidden_dev:], w_up, (((1,), (1,)), ((), ())), pr...]
    unnamed x6 -> x8, local copies, waits for them, and re-layouts: 1.55 us -> 5.71 us
  transfers between devices with their start and end apart: 2 -> 0, of which waited for: 2 -> 0; matrix products, arithmetic and copies ran while one was open for 1% -> 0% of each run, Pallas kernels for 0% -> 0%
where the time goes in v1:
time: 124 us; the launch traced here: 123 us
  Pallas kernels  113 us (91%)
  local copies, waits for them, and re-layouts  5.91 us (5%)
  other arithmetic  3.17 us (3%)
  between operations  1.34 us (1%)
    pallas_call x1, Pallas kernels, per_device(): pl.pallas_call(functools.partial(kernel, nx, nt, ny, cap, feat, hid), out...  113 us
    unnamed x8, local copies, waits for them, and re-layouts  5.71 us

profile of v1, /device:TPU:24, one launch (start us, length us, event | category | flops | bytes accessed | tf_op | source)
XLA Modules:
  0.0 123.2 jit_solution(13836964119183231776)
XLA Ops:
  0.6 0.8 pad_maximum_fusion
  1.4 0.1 reshape.9
  1.5 0.1 broadcast_select_fusion.cand_ref
  1.6 0.9 convert_reduce_fusion
  2.5 0.7 fusion.5
  3.2 0.1 broadcast_in_dim.9.col_ref
  3.9 0.1 iota.19.live_ref
  4.0 0.7 pad_maximum_fusion.1.text_ref
  4.7 0.0 copy-start
  4.7 1.5 %copy-done = bf16[1024,896]{1,0:T(8,128)(2,1)S(1)} copy-done((bf16[1024,896]{1,0:T(8,128)(2,1)S(1)}, bf16[1024,896]{1,0:T(8,128)(2,1)}, u32[]{:S(2)}) %copy-start) | copy-done | bytes 1835032
  6.2 0.0 copy-start.1
  6.2 1.5 %copy-done.1 = bf16[1024,896]{1,0:T(8,128)(2,1)S(1)} copy-done((bf16[1024,896]{1,0:T(8,128)(2,1)S(1)}, bf16[1024,896]{1,0:T(8,128)(2,1)}, u32[]{:S(2)}) %copy-start.1) | copy-done | bytes 1835032
  7.7 0.0 copy-start.2
  7.7 1.5 %copy-done.2 = bf16[896,1024]{1,0:T(8,128)(2,1)S(1)} copy-done((bf16[896,1024]{1,0:T(8,128)(2,1)S(1)}, bf16[896,1024]{1,0:T(8,128)(2,1)}, u32[]{:S(2)}) %copy-start.2) | copy-done | bytes 1835032
  9.2 112.7 %shard_map.104 = (bf16[8,1024]{1,0:T(8,128)(2,1)S(1)}, bf16[8,1024]{1,0:T(8,128)(2,1)S(1)}) custom-call(bf16[4,2,2,2048]{3,2,1,0:T(2,128)(2,1)S(1)} %broadcast_select_fusion.cand_ref, bf16[8,2048]{1,0:T(8,128)(2,1)S(1)} %pad_maximum_fusion.1.text_ref, s32[8,1024]{1,0:T(8,128)S(1)} %broadcast_in_dim.9.col_ref, s32[8,1024]{1,0:T(8,128)S(1)} %iota.19.live_ref, ...), custom_call_target="tpu_custom_call" | custom-call | tf_op jit(solution)/shard_map/pallas_call | solution.py:377
  122.0 0.6 copy.14
  122.6 0.6 copy.15
  (1 shorter events, 0.0 us)
Async XLA Ops:
  4.7 1.5 %copy-start = (bf16[1024,896]{1,0:T(8,128)(2,1)S(1)}, bf16[1024,896]{1,0:T(8,128)(2,1)}, u32[]{:S(2)}) copy-start(bf16[1024,896]{1,0:T(8,128)(2,1)} %wg_ref.1) | copy-start | bytes 5505028
  6.2 1.5 %copy-start.1 = (bf16[1024,896]{1,0:T(8,128)(2,1)S(1)}, bf16[1024,896]{1,0:T(8,128)(2,1)}, u32[]{:S(2)}) copy-start(bf16[1024,896]{1,0:T(8,128)(2,1)} %wu_ref.1) | copy-start | bytes 5505028
  7.7 1.5 %copy-start.2 = (bf16[896,1024]{1,0:T(8,128)(2,1)S(1)}, bf16[896,1024]{1,0:T(8,128)(2,1)}, u32[]{:S(2)}) copy-start(bf16[896,1024]{1,0:T(8,128)(2,1)} %wd_ref.1) | copy-start | bytes 5505028

commit v2 on v1

v2 whole, which is shorter than its diff:
```python
import functools

import jax
import jax.numpy as jnp
from jax import lax
from jax.experimental import pallas as pl
from jax.experimental.pallas import tpu as pltpu
from jax.sharding import PartitionSpec as P

MESH = pl.DeviceIdType.MESH
F32 = jnp.float32
BF16 = jnp.bfloat16
ROWS = 8
KINDS = 3
VMEM_BYTES = 67043328


def kernel(
    nx, nt, ny, cap, feat, hid,
    slot_ref, cot_ref, text_ref, tcot_ref, dest_ref, count_ref, wg_ref, wu_ref, wd_ref,
    img_ref, txt_ref,
    wg, wu, wd, cand, xr, mix, rb, xs, cs, part, mate, summed, parts_in, grads, ds, terms,
    ra_l, ra_r, sa_l, sa_r, far_a, far_a_in, got, made, held,
    wsem, xs_s, xs_r, hop_s, hop_r, mate_s, mate_r, y_s, y_r, ag_s, ag_r, fw_s, fw_r,
    a_s, a_r, b_s, b_r, f_s, f_r,
):
    ring = 2 * nt
    right_hops, left_hops = nt // 2, nt // 2 - 1
    half = nt // 4
    own = right_hops
    g, t, d = lax.axis_index("group"), lax.axis_index("tp"), lax.axis_index("dp")
    x, upper, y, c = g // 2, g % 2, d // 2, d % 2
    z = upper * nt + t

    def at(dx=0, dz=0, dy=0, flip=False):
        zz = lax.rem(z + dz + ring, ring)
        xx = lax.rem(x + dx, nx)
        yy = lax.rem(y + dy, ny)
        cc = 1 - c if flip else c
        return {"group": xx * 2 + zz // nt, "tp": lax.rem(zz, nt), "dp": yy * 2 + cc}

    started, arrived = [], []

    def send(src, dst, s, r, device):
        copy = pltpu.make_async_remote_copy(
            src, dst, s, r, device_id=device, device_id_type=MESH
        )
        copy.start()
        started.append(copy)
        return copy

    def landed(copy):
        copy.wait_recv()
        arrived.append(copy)

    loads = [
        pltpu.make_async_copy(a, b, wsem.at[i])
        for i, (a, b) in enumerate(((wg_ref, wg), (wu_ref, wu), (wd_ref, wd)))
    ]
    for load in loads:
        load.start()

    peers = [at(dx=i) for i in range(1, nx)]
    peers += [at(dy=i) for i in range(1, ny)]
    peers += [at(flip=True), at(dz=1), at(dz=-1)]
    barrier = pltpu.get_barrier_semaphore()
    for peer in peers:
        pl.semaphore_signal(barrier, inc=1, device_id=peer, device_id_type=MESH)
    for p, ref in enumerate((slot_ref, cot_ref)):
        rows = ref[...].astype(F32)
        for i in range(2 * nx):
            rel = lax.rem(i % 2 + upper, 2)
            cand[i // 2, rel, p] = rows[i * cap : i * cap + cap].astype(BF16)
    pl.semaphore_wait(barrier, len(peers))

    xcopies = []
    for i in range(1, nx):
        xcopies.append(
            send(cand.at[lax.rem(x + i, nx)], xr.at[i], xs_s.at[i], xs_r.at[i], at(dx=i))
        )

    flying = {}

    def forward(kind, p, k, way):
        sign = -1 if way == 0 else 1
        src = rb.at[own + sign * (k - 1), kind, p]
        if kind == 0 and k == 1:
            src = (text_ref, tcot_ref)[p]
        index = ((kind * 2 + p) * 2 + way) * right_hops + k - 1
        flying[kind, p, k, way] = send(
            src, rb.at[own + sign * k, kind, p], hop_s.at[index], hop_r.at[index],
            at(dz=1 if way == 0 else -1),
        )

    def arrive(k):
        for kind in range(KINDS):
            for p in range(2):
                for way in range(2):
                    last = right_hops if way == 0 else left_hops
                    if k <= last:
                        landed(flying[kind, p, k, way])
                        if k < last:
                            forward(kind, p, k + 1, way)

    for p in range(2):
        forward(0, p, 1, 0)
        forward(0, p, 1, 1)
    for copy in xcopies:
        landed(copy)
    for rel in range(2):
        for p in range(2):
            for i in range(nx):
                piece = cand[x, rel, p] if i == 0 else xr[i, rel, p]
                mix[rel, p, cap * i : cap * i + cap, :] = piece.astype(F32)
            rb[own, 1 + rel, p] = mix[rel, p].astype(BF16)
            forward(1 + rel, p, 1, 0)
            forward(1 + rel, p, 1, 1)

    def source_slots(phase):
        if phase == 0:
            return [own - half + j for j in range(2 * half)]
        return [j for j in range(half)] + [own + half + j for j in range(half)]

    def gather_rows(phase):
        slots = source_slots(phase)
        span = 2 * KINDS * ROWS
        for p, (out, first) in enumerate(((xs, text_ref), (cs, tcot_ref))):
            for q in range(half):
                pieces = []
                for s in slots[2 * q : 2 * q + 2]:
                    for kind in range(KINDS):
                        mine = s == own and kind == 0
                        pieces.append((first[...] if mine else rb[s, kind, p]).astype(F32))
                out[phase, span * q : span * q + span, :] = (
                    jnp.concatenate(pieces, axis=0).astype(BF16)
                )

    mates, ysends, gathers = {}, {}, {}

    def first_dot(phase, which):
        if which < 2:
            out = jnp.dot(xs[phase], (wg, wu)[which][...], preferred_element_type=F32)
        else:
            out = lax.dot_general(
                cs[phase], wd[...], (((1,), (1,)), ((), ())), preferred_element_type=F32
            )
        for j in range(2 * half):
            block = out[j * KINDS * ROWS : (j + 1) * KINDS * ROWS]
            part[phase, which, j % 2, j // 2] = block.reshape(KINDS, ROWS, hid).astype(BF16)
        n = phase * 3 + which
        mates[phase, which] = send(
            part.at[phase, which, 1 - c], mate.at[phase, which], mate_s.at[n], mate_r.at[n],
            at(flip=True),
        )

    def add_mate(phase, which):
        landed(mates[phase, which])
        for i in list(range(1, ny)) + [0]:
            yy = lax.rem(y + i, ny)
            total = part[phase, which, c, yy].astype(F32) + mate[phase, which, yy].astype(F32)
            summed[phase, which, i] = total.astype(BF16)
            if i:
                n = (phase * 3 + which) * ny + i
                ysends[phase, which, i] = send(
                    summed.at[phase, which, i], parts_in.at[phase, which, i],
                    y_s.at[n], y_r.at[n], at(dy=i),
                )

    def total_of(phase, which):
        total = summed[phase, which, 0].astype(F32)
        for i in range(1, ny):
            landed(ysends[phase, which, i])
            total = total + parts_in[phase, which, i].astype(F32)
        return total

    def middle(phase):
        gate = total_of(phase, 0)
        s = jax.nn.sigmoid(gate)
        slope = s * (1.0 + gate * (1.0 - s))
        up = total_of(phase, 1)
        back = total_of(phase, 2)
        grads[phase, c, y, :, :, :hid] = (back * up * slope).astype(BF16)
        grads[phase, c, y, :, :, hid:] = (back * gate * s).astype(BF16)
        mine = grads.at[phase, c, y]
        for i in range(1, ny):
            gathers[phase, i] = send(
                mine, mine, ag_s.at[phase * ny + i], ag_r.at[phase * ny + i], at(dy=i)
            )
        gathers[phase, 0] = send(
            mine, mine, fw_s.at[phase * ny], fw_r.at[phase * ny], at(flip=True)
        )

    def pass_on(phase):
        for i in range(1, ny):
            landed(gathers[phase, i])
            theirs = grads.at[phase, c, lax.rem(y - i + ny, ny)]
            gathers[phase, -i] = send(
                theirs, theirs, fw_s.at[phase * ny + i], fw_r.at[phase * ny + i], at(flip=True)
            )

    def second_dots(phase):
        for i in range(ny):
            landed(gathers[phase, -i])
        span = 2 * KINDS * ROWS
        for q in range(half):
            pieces = []
            for j in (2 * q, 2 * q + 1):
                block = grads[phase, j % 2, j // 2].astype(F32)
                pieces.append(block.reshape(KINDS * ROWS, 2 * hid))
            ds[phase, span * q : span * q + span, :] = jnp.concatenate(pieces, axis=0).astype(BF16)
        dims = (((1,), (1,)), ((), ()))
        out = lax.dot_general(ds[phase][:, :hid], wg[...], dims, preferred_element_type=F32)
        out = out + lax.dot_general(
            ds[phase][:, hid:], wu[...], dims, preferred_element_type=F32
        )
        for j in range(2 * half):
            block = out[j * KINDS * ROWS : (j + 1) * KINDS * ROWS]
            terms[phase, j] = block.reshape(KINDS, ROWS, feat).astype(BF16)

    chain = {}

    def chain_a(s):
        if s == 1:
            left, right = terms.at[0, 0], terms.at[0, 2 * half - 1]
        else:
            landed(chain["l", s - 1])
            sa_l[s - 2] = (terms[0, s - 1].astype(F32) + ra_l[s - 2].astype(F32)).astype(BF16)
            left = sa_l.at[s - 2]
            if s <= half - 1:
                landed(chain["r", s - 1])
                sa_r[s - 2] = (
                    terms[0, 2 * half - s].astype(F32) + ra_r[s - 2].astype(F32)
                ).astype(BF16)
                right = sa_r.at[s - 2]
        chain["l", s] = send(left, ra_l.at[s - 1], a_s.at[s - 1], a_r.at[s - 1], at(dz=-1))
        if s <= half - 1:
            n = half + s - 1
            chain["r", s] = send(right, ra_r.at[s - 1], a_s.at[n], a_r.at[n], at(dz=1))

    def finish_a():
        landed(chain["l", half])
        landed(chain["r", half - 1])
        total = terms[0, half].astype(F32) + ra_l[half - 1].astype(F32)
        total = total + ra_r[half - 2].astype(F32)
        far_a[...] = total[2].astype(BF16)
        chain["f"] = send(far_a, far_a_in, f_s.at[0], f_r.at[0], at(dz=2 * half))
        held[...] = total[:2]

    def chain_b(s):
        moves = (
            (2, half - s, 1, 2 * half),
            (2, half + s - 1, -1, -(2 * half + 1)),
            (0, s - 1, -1, -(half + 1)),
            (0, 2 * half - s, 1, half),
            (1, s - 1, -1, -(half + 1)),
            (1, 2 * half - s, 1, half),
        )
        for i, (kind, j, step, last) in enumerate(moves):
            if s == 1:
                src = terms.at[1, j, kind]
            else:
                landed(chain[i, s - 1])
                total = terms[1, j, kind].astype(F32) + got[i, s - 2].astype(F32)
                if s == half and i == 0:
                    landed(chain["f"])
                    total = total + far_a_in[...].astype(F32)
                made[i, s - 2] = total.astype(BF16)
                src = made.at[i, s - 2]
            n = i * half + s - 1
            chain[i, s] = send(
                src, got.at[i, s - 1], b_s.at[n], b_r.at[n], at(dz=last if s == half else step)
            )

    for k in range(1, half + 1):
        arrive(k)
    gather_rows(0)
    loads[0].wait()
    first_dot(0, 0)
    arrive(half + 1)
    loads[1].wait()
    first_dot(0, 1)
    loads[2].wait()
    first_dot(0, 2)
    for k in range(half + 2, right_hops + 1):
        arrive(k)
        if k == half + 2:
            for which in range(3):
                add_mate(0, which)
    middle(0)
    gather_rows(1)
    first_dot(1, 0)
    first_dot(1, 1)
    add_mate(1, 0)
    first_dot(1, 2)
    add_mate(1, 1)
    pass_on(0)
    add_mate(1, 2)
    second_dots(0)
    chain_a(1)
    for s in range(2, half):
        chain_a(s)
    middle(1)
    chain_a(half)
    pass_on(1)
    finish_a()
    second_dots(1)
    for s in range(1, half + 1):
        chain_b(s)
    for i in range(2, 6):
        landed(chain[i, half])
    text = held[0] + got[2, half - 1].astype(F32) + got[3, half - 1].astype(F32)
    live = lax.broadcasted_iota(jnp.int32, text.shape, 0) < count_ref[0]
    txt_ref[...] = jnp.where(live, text, 0.0).astype(BF16)
    mix[0, 0] = held[1] + got[4, half - 1].astype(F32) + got[5, half - 1].astype(F32)
    landed(chain[0, half])
    landed(chain[1, half])
    mix[0, 1] = got[0, half - 1].astype(F32) + got[1, half - 1].astype(F32)
    targets = [dest_ref[i] for i in range(ROWS)]
    for i in range(ROWS):
        rank = jnp.int32(0)
        for j in range(i):
            rank = rank + jnp.where(targets[j] == targets[i], 1, 0)
        column, away = lax.div(targets[i], 2), lax.rem(targets[i], 2)
        away = jnp.where(away == upper, 0, 1)
        row = lax.rem(x - column + nx, nx) * cap + jnp.minimum(rank, cap - 1)
        mix[1, 0, i : i + 1, :] = mix[0, away, pl.ds(row, 1), :]
    img_ref[...] = mix[1, 0].astype(BF16)
    for copy in started:
        copy.wait_send()


def per_device(
    image_slots, image_cot, text_rows, text_cot, destination, text_count, w_gate, w_up, w_down
):
    groups = lax.axis_size("group")
    nt, ndp = lax.axis_size("tp"), lax.axis_size("dp")
    nx, ny = groups // 2, ndp // 2
    slot_dev, feat = image_slots.shape
    hid = w_gate.shape[1]
    cap = slot_dev // groups
    half = nt // 4
    span = 2 * half * KINDS * ROWS
    vm, dma = pltpu.VMEM, pltpu.SemaphoreType.DMA
    block = (KINDS, ROWS, feat)
    rows = (KINDS, ROWS, hid)
    hops = nt // 2
    scratch = [
        vm((feat, hid), BF16), vm((feat, hid), BF16), vm((hid, feat), BF16),
        vm((nx, 2, 2, cap, feat), BF16), vm((nx, 2, 2, cap, feat), BF16),
        vm((2, 2, ROWS, feat), F32), vm((nt, KINDS, 2, ROWS, feat), BF16),
        vm((2, span, feat), BF16), vm((2, span, feat), BF16),
        vm((2, 3, 2, ny, *rows), BF16), vm((2, 3, ny, *rows), BF16),
        vm((2, 3, ny, *rows), BF16), vm((2, 3, ny, *rows), BF16),
        vm((2, 2, ny, KINDS, ROWS, 2 * hid), BF16), vm((2, span, 2 * hid), BF16),
        vm((2, 2 * half, *block), BF16),
        vm((half, *block), BF16), vm((half, *block), BF16),
        vm((half, *block), BF16), vm((half, *block), BF16),
        vm((ROWS, feat), BF16), vm((ROWS, feat), BF16),
        vm((6, half, ROWS, feat), BF16), vm((6, half, ROWS, feat), BF16),
        vm((2, ROWS, feat), F32),
        dma((3,)), dma((nx,)), dma((nx,)), dma((12 * hops,)), dma((12 * hops,)),
        dma((6,)), dma((6,)), dma((6 * ny,)), dma((6 * ny,)), dma((2 * ny,)), dma((2 * ny,)),
        dma((2 * ny,)), dma((2 * ny,)), dma((2 * half,)), dma((2 * half,)),
        dma((6 * half,)), dma((6 * half,)), dma((1,)), dma((1,)),
    ]
    whole = pl.BlockSpec(memory_space=pltpu.VMEM)
    apart = pl.BlockSpec(memory_space=pl.ANY)
    scalars = pl.BlockSpec(memory_space=pltpu.SMEM)
    out = jax.ShapeDtypeStruct((ROWS, feat), BF16)
    return pl.pallas_call(
        functools.partial(kernel, nx, nt, ny, cap, feat, hid),
        out_shape=(out, out),
        in_specs=[whole] * 4 + [scalars] * 2 + [apart] * 3,
        out_specs=(whole, whole),
        scratch_shapes=scratch,
        compiler_params=pltpu.CompilerParams(
            collective_id=0, has_side_effects=True, vmem_limit_bytes=VMEM_BYTES
        ),
    )(image_slots, image_cot, text_rows, text_cot, destination[:, 0], text_count,
      w_gate, w_up, w_down)


def solution(mesh):
    placed = (
        P(("group", "tp"), "dp"),
        P(("group", "tp"), "dp"),
        P(("group", "tp"), "dp"),
        P(("group", "tp"), "dp"),
        P(("group", "tp"), None),
        P(("group", "tp")),
        P("dp", "tp"),
        P("dp", "tp"),
        P("tp", "dp"),
    )
    return jax.shard_map(
        per_device,
        mesh=mesh,
        in_specs=placed,
        out_specs=(P(("group", "tp"), "dp"), P(("group", "tp"), "dp")),
        check_vma=False,
    )
```

time: 124 us -> 104 us (0.84)
  the two profiles are of different devices: /device:TPU:24 before, /device:TPU:18 now
where the time goes in v2:
time: 104 us; the launch traced here: 103 us
  Pallas kernels  99.3 us (95%)
  local copies, waits for them, and re-layouts  2.65 us (3%)
  between operations  1.29 us (1%)
    pallas_call x1, Pallas kernels, per_device(): pl.pallas_call(functools.partial(kernel, nx, nt, ny, cap, feat, hid), out...  99.3 us
    unnamed x2, local copies, waits for them, and re-layouts  2.65 us

profile of v2, /device:TPU:18, one launch (start us, length us, event | category | flops | bytes accessed | tf_op | source)
XLA Modules:
  0.0 103.3 jit_solution(665476535247606776)
XLA Ops:
  1.3 99.3 %shard_map.104 = (bf16[8,1024]{1,0:T(8,128)(2,1)}, bf16[8,1024]{1,0:T(8,128)(2,1)}) custom-call(bf16[16,1024]{1,0:T(8,128)(2,1)} %slot_ref.1, bf16[16,1024]{1,0:T(8,128)(2,1)} %cot_ref.1, bf16[8,1024]{1,0:T(8,128)(2,1)} %text_ref.1, bf16[8,1024]{1,0:T(8,128)(2,1)} %tcot_ref.1, s32[8]{0:T(128)} %bitcast.1, s32[1]{0:T(128)S(6)} %copy.13.count_ref, ...), custom_call_target="tpu_custom_call" | custom-call | tf_op jit(solution)/shard_map/pallas_call | solution.py:370
  100.6 1.3 %copy.14 = bf16[8,1024]{1,0:T(8,128)(2,1)} copy(bf16[8,1024]{1,0:T(8,128)(2,1)} %get-tuple-element.4) | data formatting | bytes 32768
  101.9 1.3 %copy.15 = bf16[8,1024]{1,0:T(8,128)(2,1)} copy(bf16[8,1024]{1,0:T(8,128)(2,1)} %get-tuple-element.5) | data formatting | bytes 32768

commit v3 on v2

--- a/solution.py
+++ b/solution.py
@@ -12,7 +12,8 @@
 BF16 = jnp.bfloat16
 ROWS = 8
 KINDS = 3
-VMEM_BYTES = 67043328
+VMEM_BYTES = 66000000
+PART = 4
 
 
 def kernel(
@@ -20,9 +21,9 @@
     slot_ref, cot_ref, text_ref, tcot_ref, dest_ref, count_ref, wg_ref, wu_ref, wd_ref,
     img_ref, txt_ref,
     wg, wu, wd, cand, xr, mix, rb, xs, cs, part, mate, summed, parts_in, grads, ds, terms,
-    ra_l, ra_r, sa_l, sa_r, far_a, far_a_in, got, made, held,
+    ra_l, ra_r, sa_l, sa_r, got, made, held,
     wsem, xs_s, xs_r, hop_s, hop_r, mate_s, mate_r, y_s, y_r, ag_s, ag_r, fw_s, fw_r,
-    a_s, a_r, b_s, b_r, f_s, f_r,
+    a_s, a_r, b_s, b_r,
 ):
     ring = 2 * nt
     right_hops, left_hops = nt // 2, nt // 2 - 1
@@ -116,16 +117,21 @@
             forward(1 + rel, p, 1, 0)
             forward(1 + rel, p, 1, 1)
 
+    def sources(phase):
+        inner = [half - 2, half - 1, half, half + 1]
+        outer = [0, 1, 2 * half - 2, 2 * half - 1]
+        return outer if phase % 2 else inner
+
     def source_slots(phase):
-        if phase == 0:
-            return [own - half + j for j in range(2 * half)]
-        return [j for j in range(half)] + [own + half + j for j in range(half)]
+        if phase < 2:
+            return [own - half + j for j in sources(phase)]
+        return [j if j < half else own + j for j in sources(phase)]
 
     def gather_rows(phase):
         slots = source_slots(phase)
         span = 2 * KINDS * ROWS
         for p, (out, first) in enumerate(((xs, text_ref), (cs, tcot_ref))):
-            for q in range(half):
+            for q in range(half // 2):
                 pieces = []
                 for s in slots[2 * q : 2 * q + 2]:
                     for kind in range(KINDS):
@@ -144,9 +150,10 @@
             out = lax.dot_general(
                 cs[phase], wd[...], (((1,), (1,)), ((), ())), preferred_element_type=F32
             )
-        for j in range(2 * half):
-            block = out[j * KINDS * ROWS : (j + 1) * KINDS * ROWS]
-            part[phase, which, j % 2, j // 2] = block.reshape(KINDS, ROWS, hid).astype(BF16)
+        for i in range(ny):
+            block = out[i * KINDS * ROWS : (i + 1) * KINDS * ROWS].reshape(KINDS, ROWS, hid)
+            for core in range(2):
+                part[phase, which, core, i] = block[:, core * PART : core * PART + PART].astype(BF16)
         n = phase * 3 + which
         mates[phase, which] = send(
             part.at[phase, which, 1 - c], mate.at[phase, which], mate_s.at[n], mate_r.at[n],
@@ -202,10 +209,12 @@
         for i in range(ny):
             landed(gathers[phase, -i])
         span = 2 * KINDS * ROWS
-        for q in range(half):
+        for q in range(half // 2):
             pieces = []
-            for j in (2 * q, 2 * q + 1):
-                block = grads[phase, j % 2, j // 2].astype(F32)
+            for i in (2 * q, 2 * q + 1):
+                block = jnp.concatenate(
+                    [grads[phase, core, i].astype(F32) for core in range(2)], axis=1
+                )
                 pieces.append(block.reshape(KINDS * ROWS, 2 * hid))
             ds[phase, span * q : span * q + span, :] = jnp.concatenate(pieces, axis=0).astype(BF16)
         dims = (((1,), (1,)), ((), ()))
@@ -213,23 +222,24 @@
         out = out + lax.dot_general(
             ds[phase][:, hid:], wu[...], dims, preferred_element_type=F32
         )
-        for j in range(2 * half):
-            block = out[j * KINDS * ROWS : (j + 1) * KINDS * ROWS]
-            terms[phase, j] = block.reshape(KINDS, ROWS, feat).astype(BF16)
+        for i, j in enumerate(sources(phase)):
+            block = out[i * KINDS * ROWS : (i + 1) * KINDS * ROWS]
+            terms[phase // 2, j] = block.reshape(KINDS, ROWS, feat).astype(BF16)
 
     chain = {}
+    two = slice(0, 2)
 
     def chain_a(s):
         if s == 1:
-            left, right = terms.at[0, 0], terms.at[0, 2 * half - 1]
+            left, right = terms.at[0, 0, two], terms.at[0, 2 * half - 1, two]
         else:
             landed(chain["l", s - 1])
-            sa_l[s - 2] = (terms[0, s - 1].astype(F32) + ra_l[s - 2].astype(F32)).astype(BF16)
+            sa_l[s - 2] = (terms[0, s - 1, two].astype(F32) + ra_l[s - 2].astype(F32)).astype(BF16)
             left = sa_l.at[s - 2]
             if s <= half - 1:
                 landed(chain["r", s - 1])
                 sa_r[s - 2] = (
-                    terms[0, 2 * half - s].astype(F32) + ra_r[s - 2].astype(F32)
+                    terms[0, 2 * half - s, two].astype(F32) + ra_r[s - 2].astype(F32)
                 ).astype(BF16)
                 right = sa_r.at[s - 2]
         chain["l", s] = send(left, ra_l.at[s - 1], a_s.at[s - 1], a_r.at[s - 1], at(dz=-1))
@@ -240,81 +250,117 @@
     def finish_a():
         landed(chain["l", half])
         landed(chain["r", half - 1])
-        total = terms[0, half].astype(F32) + ra_l[half - 1].astype(F32)
-        total = total + ra_r[half - 2].astype(F32)
-        far_a[...] = total[2].astype(BF16)
-        chain["f"] = send(far_a, far_a_in, f_s.at[0], f_r.at[0], at(dz=2 * half))
-        held[...] = total[:2]
-
-    def chain_b(s):
-        moves = (
-            (2, half - s, 1, 2 * half),
-            (2, half + s - 1, -1, -(2 * half + 1)),
-            (0, s - 1, -1, -(half + 1)),
-            (0, 2 * half - s, 1, half),
-            (1, s - 1, -1, -(half + 1)),
-            (1, 2 * half - s, 1, half),
-        )
-        for i, (kind, j, step, last) in enumerate(moves):
-            if s == 1:
-                src = terms.at[1, j, kind]
-            else:
-                landed(chain[i, s - 1])
-                total = terms[1, j, kind].astype(F32) + got[i, s - 2].astype(F32)
-                if s == half and i == 0:
-                    landed(chain["f"])
-                    total = total + far_a_in[...].astype(F32)
-                made[i, s - 2] = total.astype(BF16)
-                src = made.at[i, s - 2]
-            n = i * half + s - 1
-            chain[i, s] = send(
-                src, got.at[i, s - 1], b_s.at[n], b_r.at[n], at(dz=last if s == half else step)
-            )
-
-    for k in range(1, half + 1):
-        arrive(k)
-    gather_rows(0)
-    loads[0].wait()
-    first_dot(0, 0)
-    arrive(half + 1)
-    loads[1].wait()
-    first_dot(0, 1)
-    loads[2].wait()
-    first_dot(0, 2)
-    for k in range(half + 2, right_hops + 1):
-        arrive(k)
-        if k == half + 2:
-            for which in range(3):
-                add_mate(0, which)
+        total = terms[0, half, two].astype(F32) + ra_l[half - 1].astype(F32)
+        held[...] = total + ra_r[half - 2].astype(F32)
+
+    far_r = [(0, half - k, 1) for k in range(half + 1)]
+    far_r += [(1, 2 * half - k, 1) for k in range(half + 1, 2 * half)] + [(1, 0, 2 * half)]
+    far_l = [(0, half + k, -1) for k in range(1, half)]
+    far_l += [(1, k, -1) for k in range(half, 2 * half - 1)] + [(1, 2 * half - 1, -(2 * half + 1))]
+    inner_l = [(1, half - 2, -1), (1, half - 1, -(half + 1))]
+    inner_r = [(1, half + 1, 1), (1, half, half)]
+    outer_l = [(1, 0, -1), (1, 1, -(2 * half - 1))]
+    outer_r = [(1, 2 * half - 1, 1), (1, 2 * half - 2, 2 * half - 2)]
+    routes = [(2, far_r), (2, far_l)]
+    routes += [(kind, way) for way in (inner_l, inner_r, outer_l, outer_r) for kind in (0, 1)]
+    first = [sum(len(r[1]) for r in routes[:i]) for i in range(len(routes))]
+
+    def hop_on(i, s):
+        kind, steps = routes[i]
+        ab, j, dz = steps[s - 1]
+        n = first[i] + s - 1
+        if s == 1:
+            src = terms.at[ab, j, kind]
+        else:
+            landed(chain[i, s - 1])
+            made[n] = (terms[ab, j, kind].astype(F32) + got[n - 1].astype(F32)).astype(BF16)
+            src = made.at[n]
+        chain[i, s] = send(src, got.at[n], b_s.at[n], b_r.at[n], at(dz=dz))
+
+    def ended(i):
+        landed(chain[i, len(routes[i][1])])
+        return got[first[i] + len(routes[i][1]) - 1].astype(F32)
+
+    def dots(phase):
+        gather_rows(phase)
+        for which in range(3):
+            if phase == 0:
+                loads[which].wait()
+            first_dot(phase, which)
+
+    def add_mates(phase):
+        for which in range(3):
+            add_mate(phase, which)
+
+    arrive(1)
+    arrive(2)
+    dots(0)
+    arrive(3)
+    add_mates(0)
+    arrive(4)
+    dots(1)
+    arrive(5)
+    add_mates(1)
     middle(0)
-    gather_rows(1)
-    first_dot(1, 0)
-    first_dot(1, 1)
-    add_mate(1, 0)
-    first_dot(1, 2)
-    add_mate(1, 1)
+    arrive(6)
+    dots(2)
     pass_on(0)
-    add_mate(1, 2)
+    arrive(7)
+    add_mates(2)
+    middle(1)
     second_dots(0)
+    hop_on(0, 1)
+    hop_on(1, 1)
+    arrive(8)
+    gather_rows(3)
+    first_dot(3, 0)
+    first_dot(3, 1)
+    hop_on(0, 2)
+    add_mate(3, 0)
+    first_dot(3, 2)
+    add_mate(3, 1)
+    pass_on(1)
+    add_mate(3, 2)
+    middle(2)
+    hop_on(0, 3)
+    second_dots(1)
     chain_a(1)
-    for s in range(2, half):
-        chain_a(s)
-    middle(1)
-    chain_a(half)
-    pass_on(1)
+    hop_on(0, 4)
+    hop_on(1, 2)
+    pass_on(2)
+    chain_a(2)
+    middle(3)
+    hop_on(0, 5)
+    hop_on(1, 3)
+    second_dots(2)
+    for i in range(2, 6):
+        hop_on(i, 1)
+    hop_on(0, 6)
+    hop_on(1, 4)
+    chain_a(3)
+    pass_on(3)
+    hop_on(0, 7)
+    hop_on(1, 5)
+    second_dots(3)
+    for i in range(6, 10):
+        hop_on(i, 1)
+    hop_on(0, 8)
+    hop_on(1, 6)
+    chain_a(4)
+    for i in range(2, 6):
+        hop_on(i, 2)
+    hop_on(0, 9)
+    hop_on(1, 7)
+    for i in range(6, 10):
+        hop_on(i, 2)
     finish_a()
-    second_dots(1)
-    for s in range(1, half + 1):
-        chain_b(s)
-    for i in range(2, 6):
-        landed(chain[i, half])
-    text = held[0] + got[2, half - 1].astype(F32) + got[3, half - 1].astype(F32)
-    live = lax.broadcasted_iota(jnp.int32, text.shape, 0) < count_ref[0]
-    txt_ref[...] = jnp.where(live, text, 0.0).astype(BF16)
-    mix[0, 0] = held[1] + got[4, half - 1].astype(F32) + got[5, half - 1].astype(F32)
-    landed(chain[0, half])
-    landed(chain[1, half])
-    mix[0, 1] = got[0, half - 1].astype(F32) + got[1, half - 1].astype(F32)
+    sums = [held[0], held[1]]
+    for i in range(2, 10):
+        sums[i % 2] = sums[i % 2] + ended(i)
+    live = lax.broadcasted_iota(jnp.int32, sums[0].shape, 0) < count_ref[0]
+    txt_ref[...] = jnp.where(live, sums[0], 0.0).astype(BF16)
+    mix[0, 0] = sums[1]
+    mix[0, 1] = ended(0) + ended(1)
     targets = [dest_ref[i] for i in range(ROWS)]
     for i in range(ROWS):
         rank = jnp.int32(0)
@@ -339,29 +385,28 @@
     hid = w_gate.shape[1]
     cap = slot_dev // groups
     half = nt // 4
-    span = 2 * half * KINDS * ROWS
     vm, dma = pltpu.VMEM, pltpu.SemaphoreType.DMA
     block = (KINDS, ROWS, feat)
-    rows = (KINDS, ROWS, hid)
+    rows = (KINDS, PART, hid)
     hops = nt // 2
+    span = half * KINDS * ROWS
+    pair = (half, 2, ROWS, feat)
     scratch = [
         vm((feat, hid), BF16), vm((feat, hid), BF16), vm((hid, feat), BF16),
         vm((nx, 2, 2, cap, feat), BF16), vm((nx, 2, 2, cap, feat), BF16),
         vm((2, 2, ROWS, feat), F32), vm((nt, KINDS, 2, ROWS, feat), BF16),
-        vm((2, span, feat), BF16), vm((2, span, feat), BF16),
-        vm((2, 3, 2, ny, *rows), BF16), vm((2, 3, ny, *rows), BF16),
-        vm((2, 3, ny, *rows), BF16), vm((2, 3, ny, *rows), BF16),
-        vm((2, 2, ny, KINDS, ROWS, 2 * hid), BF16), vm((2, span, 2 * hid), BF16),
+        vm((4, span, feat), BF16), vm((4, span, feat), BF16),
+        vm((4, 3, 2, ny, *rows), BF16), vm((4, 3, ny, *rows), BF16),
+        vm((4, 3, ny, *rows), BF16), vm((4, 3, ny, *rows), BF16),
+        vm((4, 2, ny, KINDS, PART, 2 * hid), BF16), vm((4, span, 2 * hid), BF16),
         vm((2, 2 * half, *block), BF16),
-        vm((half, *block), BF16), vm((half, *block), BF16),
-        vm((half, *block), BF16), vm((half, *block), BF16),
-        vm((ROWS, feat), BF16), vm((ROWS, feat), BF16),
-        vm((6, half, ROWS, feat), BF16), vm((6, half, ROWS, feat), BF16),
+        vm(pair, BF16), vm(pair, BF16), vm(pair, BF16), vm(pair, BF16),
+        vm((32, ROWS, feat), BF16), vm((32, ROWS, feat), BF16),
         vm((2, ROWS, feat), F32),
         dma((3,)), dma((nx,)), dma((nx,)), dma((12 * hops,)), dma((12 * hops,)),
-        dma((6,)), dma((6,)), dma((6 * ny,)), dma((6 * ny,)), dma((2 * ny,)), dma((2 * ny,)),
-        dma((2 * ny,)), dma((2 * ny,)), dma((2 * half,)), dma((2 * half,)),
-        dma((6 * half,)), dma((6 * half,)), dma((1,)), dma((1,)),
+        dma((12,)), dma((12,)), dma((12 * ny,)), dma((12 * ny,)), dma((4 * ny,)), dma((4 * ny,)),
+        dma((4 * ny,)), dma((4 * ny,)), dma((2 * half,)), dma((2 * half,)),
+        dma((32,)), dma((32,)),
     ]
     whole = pl.BlockSpec(memory_space=pltpu.VMEM)
     apart = pl.BlockSpec(memory_space=pl.ANY)

time: 104 us -> 95.4 us (0.917)
  the two profiles are of different devices: /device:TPU:18 before, /device:TPU:2 now
where the time goes in v3:
time: 95.4 us; the launch traced here: 95.1 us
  Pallas kernels  91.2 us (96%)
  local copies, waits for them, and re-layouts  2.65 us (3%)
  between operations  1.29 us (1%)
    pallas_call x1, Pallas kernels, per_device(): pl.pallas_call(functools.partial(kernel, nx, nt, ny, cap, feat, hid), out...  91.2 us
    unnamed x2, local copies, waits for them, and re-layouts  2.65 us

profile of v3, /device:TPU:2, one launch (start us, length us, event | category | flops | bytes accessed | tf_op | source)
XLA Modules:
  0.0 95.1 jit_solution(1892229332547340255)
XLA Ops:
  1.3 91.2 %shard_map.104 = (bf16[8,1024]{1,0:T(8,128)(2,1)}, bf16[8,1024]{1,0:T(8,128)(2,1)}) custom-call(bf16[16,1024]{1,0:T(8,128)(2,1)} %slot_ref.1, bf16[16,1024]{1,0:T(8,128)(2,1)} %cot_ref.1, bf16[8,1024]{1,0:T(8,128)(2,1)} %text_ref.1, bf16[8,1024]{1,0:T(8,128)(2,1)} %tcot_ref.1, s32[8]{0:T(128)} %bitcast.1, s32[1]{0:T(128)S(6)} %copy.13.count_ref, ...), custom_call_target="tpu_custom_call" | custom-call | tf_op jit(solution)/shard_map/pallas_call | solution.py:415
  92.4 1.3 %copy.14 = bf16[8,1024]{1,0:T(8,128)(2,1)} copy(bf16[8,1024]{1,0:T(8,128)(2,1)} %get-tuple-element.4) | data formatting | bytes 32768
  93.8 1.3 %copy.15 = bf16[8,1024]{1,0:T(8,128)(2,1)} copy(bf16[8,1024]{1,0:T(8,128)(2,1)} %get-tuple-element.5) | data formatting | bytes 32768

commit v4 on v3

--- a/solution.py
+++ b/solution.py
@@ -19,7 +19,7 @@
 def kernel(
     nx, nt, ny, cap, feat, hid,
     slot_ref, cot_ref, text_ref, tcot_ref, dest_ref, count_ref, wg_ref, wu_ref, wd_ref,
-    img_ref, txt_ref,
+    out_ref,
     wg, wu, wd, cand, xr, mix, rb, xs, cs, part, mate, summed, parts_in, grads, ds, terms,
     ra_l, ra_r, sa_l, sa_r, got, made, held,
     wsem, xs_s, xs_r, hop_s, hop_r, mate_s, mate_r, y_s, y_r, ag_s, ag_r, fw_s, fw_r,
@@ -63,7 +63,7 @@
 
     peers = [at(dx=i) for i in range(1, nx)]
     peers += [at(dy=i) for i in range(1, ny)]
-    peers += [at(flip=True), at(dz=1), at(dz=-1)]
+    peers += [at(flip=True), at(dz=1), at(dz=-1), at(dz=2), at(dz=-2)]
     barrier = pltpu.get_barrier_semaphore()
     for peer in peers:
         pl.semaphore_signal(barrier, inc=1, device_id=peer, device_id_type=MESH)
@@ -84,14 +84,20 @@
 
     def forward(kind, p, k, way):
         sign = -1 if way == 0 else 1
-        src = rb.at[own + sign * (k - 1), kind, p]
-        if kind == 0 and k == 1:
+        hops = k if k < 3 else 1
+        src = rb.at[own + sign * (k - hops), kind, p]
+        if kind == 0 and k < 3:
             src = (text_ref, tcot_ref)[p]
         index = ((kind * 2 + p) * 2 + way) * right_hops + k - 1
         flying[kind, p, k, way] = send(
             src, rb.at[own + sign * k, kind, p], hop_s.at[index], hop_r.at[index],
-            at(dz=1 if way == 0 else -1),
-        )
+            at(dz=hops if way == 0 else -hops),
+        )
+
+    def begin(kind, p):
+        for k in (2, 1):
+            forward(kind, p, k, 0)
+            forward(kind, p, k, 1)
 
     def arrive(k):
         for kind in range(KINDS):
@@ -100,12 +106,11 @@
                     last = right_hops if way == 0 else left_hops
                     if k <= last:
                         landed(flying[kind, p, k, way])
-                        if k < last:
+                        if 1 < k < last:
                             forward(kind, p, k + 1, way)
 
     for p in range(2):
-        forward(0, p, 1, 0)
-        forward(0, p, 1, 1)
+        begin(0, p)
     for copy in xcopies:
         landed(copy)
     for rel in range(2):
@@ -114,8 +119,7 @@
                 piece = cand[x, rel, p] if i == 0 else xr[i, rel, p]
                 mix[rel, p, cap * i : cap * i + cap, :] = piece.astype(F32)
             rb[own, 1 + rel, p] = mix[rel, p].astype(BF16)
-            forward(1 + rel, p, 1, 0)
-            forward(1 + rel, p, 1, 1)
+            begin(1 + rel, p)
 
     def sources(phase):
         inner = [half - 2, half - 1, half, half + 1]
@@ -253,16 +257,17 @@
         total = terms[0, half, two].astype(F32) + ra_l[half - 1].astype(F32)
         held[...] = total + ra_r[half - 2].astype(F32)
 
-    far_r = [(0, half - k, 1) for k in range(half + 1)]
-    far_r += [(1, 2 * half - k, 1) for k in range(half + 1, 2 * half)] + [(1, 0, 2 * half)]
-    far_l = [(0, half + k, -1) for k in range(1, half)]
-    far_l += [(1, k, -1) for k in range(half, 2 * half - 1)] + [(1, 2 * half - 1, -(2 * half + 1))]
+    far_r = [(0, half - k, 1) for k in range(half)] + [(0, 0, half)]
+    far_l = [(0, half + k, -1) for k in range(1, half - 1)] + [(0, 2 * half - 1, -half)]
+    end_r = [(1, half - k, 1) for k in range(1, half)] + [(1, 0, 2 * half)]
+    end_l = [(1, half + k, -1) for k in range(half - 1)] + [(1, 2 * half - 1, -(2 * half + 1))]
     inner_l = [(1, half - 2, -1), (1, half - 1, -(half + 1))]
     inner_r = [(1, half + 1, 1), (1, half, half)]
     outer_l = [(1, 0, -1), (1, 1, -(2 * half - 1))]
     outer_r = [(1, 2 * half - 1, 1), (1, 2 * half - 2, 2 * half - 2)]
     routes = [(2, far_r), (2, far_l)]
     routes += [(kind, way) for way in (inner_l, inner_r, outer_l, outer_r) for kind in (0, 1)]
+    routes += [(2, end_r), (2, end_l)]
     first = [sum(len(r[1]) for r in routes[:i]) for i in range(len(routes))]
 
     def hop_on(i, s):
@@ -273,7 +278,10 @@
             src = terms.at[ab, j, kind]
         else:
             landed(chain[i, s - 1])
-            made[n] = (terms[ab, j, kind].astype(F32) + got[n - 1].astype(F32)).astype(BF16)
+            total = terms[ab, j, kind].astype(F32) + got[n - 1].astype(F32)
+            if i >= 10 and s == len(steps):
+                total = total + ended(i - 10)
+            made[n] = total.astype(BF16)
             src = made.at[n]
         chain[i, s] = send(src, got.at[n], b_s.at[n], b_r.at[n], at(dz=dz))
 
@@ -315,52 +323,52 @@
     gather_rows(3)
     first_dot(3, 0)
     first_dot(3, 1)
-    hop_on(0, 2)
     add_mate(3, 0)
     first_dot(3, 2)
     add_mate(3, 1)
+    hop_on(0, 2)
     pass_on(1)
     add_mate(3, 2)
     middle(2)
-    hop_on(0, 3)
     second_dots(1)
     chain_a(1)
+    hop_on(0, 3)
+    hop_on(1, 2)
+    chain_a(2)
     hop_on(0, 4)
-    hop_on(1, 2)
+    hop_on(1, 3)
     pass_on(2)
-    chain_a(2)
     middle(3)
-    hop_on(0, 5)
-    hop_on(1, 3)
     second_dots(2)
+    hop_on(10, 1)
+    hop_on(11, 1)
     for i in range(2, 6):
         hop_on(i, 1)
-    hop_on(0, 6)
-    hop_on(1, 4)
+    hop_on(0, 5)
     chain_a(3)
     pass_on(3)
-    hop_on(0, 7)
-    hop_on(1, 5)
+    hop_on(10, 2)
+    hop_on(11, 2)
+    for i in range(2, 6):
+        hop_on(i, 2)
     second_dots(3)
     for i in range(6, 10):
         hop_on(i, 1)
-    hop_on(0, 8)
-    hop_on(1, 6)
+    hop_on(10, 3)
+    hop_on(11, 3)
     chain_a(4)
-    for i in range(2, 6):
-        hop_on(i, 2)
-    hop_on(0, 9)
-    hop_on(1, 7)
     for i in range(6, 10):
         hop_on(i, 2)
+    hop_on(10, 4)
+    hop_on(11, 4)
     finish_a()
     sums = [held[0], held[1]]
     for i in range(2, 10):
         sums[i % 2] = sums[i % 2] + ended(i)
     live = lax.broadcasted_iota(jnp.int32, sums[0].shape, 0) < count_ref[0]
-    txt_ref[...] = jnp.where(live, sums[0], 0.0).astype(BF16)
+    out_ref[1] = jnp.where(live, sums[0], 0.0).astype(BF16)
     mix[0, 0] = sums[1]
-    mix[0, 1] = ended(0) + ended(1)
+    mix[0, 1] = ended(10) + ended(11)
     targets = [dest_ref[i] for i in range(ROWS)]
     for i in range(ROWS):
         rank = jnp.int32(0)
@@ -370,7 +378,7 @@
         away = jnp.where(away == upper, 0, 1)
         row = lax.rem(x - column + nx, nx) * cap + jnp.minimum(rank, cap - 1)
         mix[1, 0, i : i + 1, :] = mix[0, away, pl.ds(row, 1), :]
-    img_ref[...] = mix[1, 0].astype(BF16)
+    out_ref[0] = mix[1, 0].astype(BF16)
     for copy in started:
         copy.wait_send()
 
@@ -411,18 +419,19 @@
     whole = pl.BlockSpec(memory_space=pltpu.VMEM)
     apart = pl.BlockSpec(memory_space=pl.ANY)
     scalars = pl.BlockSpec(memory_space=pltpu.SMEM)
-    out = jax.ShapeDtypeStruct((ROWS, feat), BF16)
-    return pl.pallas_call(
+    out = jax.ShapeDtypeStruct((2, ROWS, feat), BF16)
+    grads = pl.pallas_call(
         functools.partial(kernel, nx, nt, ny, cap, feat, hid),
-        out_shape=(out, out),
+        out_shape=out,
         in_specs=[whole] * 4 + [scalars] * 2 + [apart] * 3,
-        out_specs=(whole, whole),
+        out_specs=whole,
         scratch_shapes=scratch,
         compiler_params=pltpu.CompilerParams(
             collective_id=0, has_side_effects=True, vmem_limit_bytes=VMEM_BYTES
         ),
     )(image_slots, image_cot, text_rows, text_cot, destination[:, 0], text_count,
       w_gate, w_up, w_down)
+    return grads[0], grads[1]
 
 
 def solution(mesh):

time: 95.4 us -> 93.9 us (0.984)
  the two profiles are of different devices: /device:TPU:2 before, /device:TPU:24 now
where the time goes in v4:
time: 93.9 us; the launch traced here: 92.1 us
  Pallas kernels  89.5 us (95%)
  local copies, waits for them, and re-layouts  1.35 us (1%)
  between operations  1.29 us (1%)
    pallas_call x1, Pallas kernels, per_device(): pl.pallas_call(functools.partial(kernel, nx, nt, ny, cap, feat, hid), out...  89.5 us

profile of v4, /device:TPU:24, one launch (start us, length us, event | category | flops | bytes accessed | tf_op | source)
XLA Modules:
  0.0 92.1 jit_solution(8665520887536242314)
XLA Ops:
  1.3 89.5 %shard_map.104 = bf16[2,8,1024]{2,1,0:T(8,128)(2,1)} custom-call(bf16[16,1024]{1,0:T(8,128)(2,1)} %slot_ref.1, bf16[16,1024]{1,0:T(8,128)(2,1)} %cot_ref.1, bf16[8,1024]{1,0:T(8,128)(2,1)} %text_ref.1, bf16[8,1024]{1,0:T(8,128)(2,1)} %tcot_ref.1, s32[8]{0:T(128)} %bitcast.5, s32[1]{0:T(128)S(6)} %copy.11.count_ref, bf16[1024,896]{1,0:T(8,128)(2,1)} %wg_ref.1, ...), custom_call_target="tpu_custom_call" | custom-call | tf_op jit(solution)/shard_map/pallas_call | solution.py:423
  90.8 1.3 %slice_bitcast_fusion = (bf16[8,1024]{1,0:T(8,128)(2,1)}, bf16[8,1024]{1,0:T(8,128)(2,1)}) fusion(bf16[2,8,1024]{2,1,0:T(8,128)(2,1)} %shard_map.104), kind=kLoop, calls=%fused_computation | loop fusion | bytes 65536 | tf_op jit(solution)/shard_map/squeeze | solution.py:434

commit v5 on v4

--- a/solution.py
+++ b/solution.py
@@ -309,16 +309,13 @@
     dots(1)
     arrive(5)
     add_mates(1)
+    arrive(6)
     middle(0)
-    arrive(6)
     dots(2)
-    pass_on(0)
     arrive(7)
     add_mates(2)
+    pass_on(0)
     middle(1)
-    second_dots(0)
-    hop_on(0, 1)
-    hop_on(1, 1)
     arrive(8)
     gather_rows(3)
     first_dot(3, 0)
@@ -326,31 +323,34 @@
     add_mate(3, 0)
     first_dot(3, 2)
     add_mate(3, 1)
-    hop_on(0, 2)
+    second_dots(0)
+    hop_on(0, 1)
+    hop_on(1, 1)
+    add_mate(3, 2)
     pass_on(1)
-    add_mate(3, 2)
     middle(2)
     second_dots(1)
     chain_a(1)
-    hop_on(0, 3)
+    hop_on(0, 2)
     hop_on(1, 2)
     chain_a(2)
-    hop_on(0, 4)
-    hop_on(1, 3)
     pass_on(2)
     middle(3)
+    hop_on(0, 3)
+    hop_on(1, 3)
     second_dots(2)
     hop_on(10, 1)
     hop_on(11, 1)
     for i in range(2, 6):
         hop_on(i, 1)
-    hop_on(0, 5)
+    hop_on(0, 4)
     chain_a(3)
     pass_on(3)
     hop_on(10, 2)
     hop_on(11, 2)
     for i in range(2, 6):
         hop_on(i, 2)
+    hop_on(0, 5)
     second_dots(3)
     for i in range(6, 10):
         hop_on(i, 1)

time: 93.9 us -> 95.1 us (1.013)
  Pallas kernels: 89.5 us -> 90.7 us
    pallas_call x1, Pallas kernels: 89.5 us -> 90.7 us  [per_device(): pl.pallas_call(functools.partial(kernel, nx, nt, ny, cap, feat, hid), out...]
where the time goes in v5:
time: 95.1 us; the launch traced here: 93.4 us
  Pallas kernels  90.7 us (95%)
  local copies, waits for them, and re-layouts  1.35 us (1%)
  between operations  1.29 us (1%)
    pallas_call x1, Pallas kernels, per_device(): pl.pallas_call(functools.partial(kernel, nx, nt, ny, cap, feat, hid), out...  90.7 us

profile of v5, /device:TPU:24, one launch (start us, length us, event | category | flops | bytes accessed | tf_op | source)
XLA Modules:
  0.0 93.4 jit_solution(13137270018985884517)
XLA Ops:
  1.3 90.7 %shard_map.104 = bf16[2,8,1024]{2,1,0:T(8,128)(2,1)} custom-call(bf16[16,1024]{1,0:T(8,128)(2,1)} %slot_ref.1, bf16[16,1024]{1,0:T(8,128)(2,1)} %cot_ref.1, bf16[8,1024]{1,0:T(8,128)(2,1)} %text_ref.1, bf16[8,1024]{1,0:T(8,128)(2,1)} %tcot_ref.1, s32[8]{0:T(128)} %bitcast.5, s32[1]{0:T(128)S(6)} %copy.11.count_ref, bf16[1024,896]{1,0:T(8,128)(2,1)} %wg_ref.1, ...), custom_call_target="tpu_custom_call" | custom-call | tf_op jit(solution)/shard_map/pallas_call | solution.py:423
  92.0 1.3 %slice_bitcast_fusion = (bf16[8,1024]{1,0:T(8,128)(2,1)}, bf16[8,1024]{1,0:T(8,128)(2,1)}) fusion(bf16[2,8,1024]{2,1,0:T(8,128)(2,1)} %shard_map.104), kind=kLoop, calls=%fused_computation | loop fusion | bytes 65536 | tf_op jit(solution)/shard_map/squeeze | solution.py:434
